TPU v7x, 32 devices: a whole 2x2x4 slice. The times are simulated.
32 devices in a mesh: ex: 8 (over z, x), feat: 4 (over y, core).
Axes of the slice: x: 2, y: 2, z: 4, core: 2. Of those that a mesh axis runs over, the one named last changes fastest.
Arguments:
- train_grads: bfloat16 [3072, 16384], P('ex', 'feat'), may hold values from -6 to 6
- projection: bfloat16 [16384, 4096], P('feat', 'ex'), may hold values from -0.046875 to 0.046875
- test_features: bfloat16 [256, 4096], P('ex', 'feat'), may hold values from -0.09375 to 0.09375
- example_weights: float32 [3072], P('ex'), may hold values from 0.05 to 1
Outputs:
- scores: float32 [256, 3072], P('feat', 'ex')
- projected: bfloat16 [3072, 4096], P('ex', 'feat')
All inputs are finite; a program needn't handle non-finite values.
Results may differ from a plain program's by a relative error of at most 0.0031.
Values may be sent and summed in bfloat16 or wider, within the bound.
No kernel may reach another device: no remote copies, remote signals or barrier semaphores. Data moves between devices by JAX's collectives and lax.ppermute only.
A program may use at most 192 MiB of HBM per device.

v0:
```python
import jax
import jax.numpy as jnp
from jax import lax
from jax.sharding import PartitionSpec as P


def local(train_grads, projection, test_features, example_weights):
    columns = jnp.dot(
        lax.all_gather(train_grads, "ex", axis=0, tiled=True),
        projection,
        preferred_element_type=jnp.float32,
    )
    partial_value = lax.all_to_all(columns, "ex", split_axis=0, concat_axis=1, tiled=True)
    projected = lax.psum_scatter(partial_value, "feat", scatter_dimension=1, tiled=True).astype(
        jnp.bfloat16
    )
    partial_scores = lax.dot_general(
        lax.all_gather(test_features, "ex", axis=0, tiled=True),
        projected,
        (((1,), (1,)), ((), ())),
        preferred_element_type=jnp.float32,
    )
    inner = lax.psum_scatter(partial_scores, "feat", scatter_dimension=0, tiled=True)
    return (inner * example_weights[None, :], projected)


def solution(mesh):
    return jax.shard_map(
        local,
        mesh=mesh,
        in_specs=(P("ex", "feat"), P("feat", "ex"), P("ex", "feat"), P("ex")),
        out_specs=(P("feat", "ex"), P("ex", "feat")),
        check_vma=False,
    )
```

profile of v0, /device:TPU:0, one launch (start us, length us, event | category | flops | bytes accessed | tf_op | source)
XLA Modules:
  0.0 745.7 jit_solution(3920814526854511127)
XLA Ops:
  7.2 0.0 all-gather.2.cloned.1.call-start
  7.2 0.7 all-gather.2.cloned.1.call-update
  7.9 0.0 reduce-scatter.5.cloned.1.call-start
  7.9 484.7 %all-gather.2.cloned.1.call-done = bf16[3072,4096]{1,0:T(8,128)(2,1)} async-done(((bf16[384,4096]{1,0:T(8,128)(2,1)}), bf16[3072,4096]{1,0:T(8,128)(2,1)}) %all-gather.2.cloned.1.call-update) | async-done | bytes 25165840 | tf_op jit(solution)/shard_map/all_gather | solution.py:9
  492.6 17.7 %fusion = f32[3072,512]{1,0:T(8,128)S(1)} fusion(bf16[3072,4096]{1,0:T(8,128)(2,1)} %all-gather.2.cloned.1.call-done, bf16[4096,512]{1,0:T(8,128)(2,1)} %param.5), kind=kOutput, calls=%fused_computation.2 | convolution fusion | flops 12884901888 | bytes 35651584 | tf_op jit(solution)/shard_map/dot_general | solution.py:8
  510.3 142.6 %all_to_all.19 = f32[8,384,512]{2,1,0:T(8,128)S(1)} all-to-all(f32[8,384,512]{2,1,0:T(8,128)S(1)} %bitcast.13), channel_id=1, replica_groups=mesh['ex'=8,'feat'=4] {'ex'}, dimensions={0} | all-to-all | bytes 12582912 | tf_op jit(solution)/shard_map/all_to_all | solution.py:13
  652.9 3.4 copy.12
  656.3 0.0 copy-start.1
  656.3 0.0 copy-start.2
  656.3 0.0 reduce-scatter.5.cloned.1.call-update
  656.3 0.0 reduce-scatter.7.cloned.1.call-start
  656.4 0.8 copy-done.1
  657.1 31.6 %all_gather.7 = bf16[256,1024]{1,0:T(8,128)(2,1)S(1)} all-gather(bf16[32,1024]{1,0:T(8,128)(2,1)S(1)} %copy-done.1), channel_id=1, replica_groups=mesh['ex'=8,'feat'=4] {'ex'}, dimensions={0}, use_global_device_ids=true | all-gather | bytes 589824 | tf_op jit(solution)/shard_map/all_gather | solution.py:18
  688.7 24.7 %reduce-scatter.5.cloned.1.call-done = f32[384,1024]{1,0:T(8,128)} async-done(((f32[384,4096]{1,0:T(8,128)}), f32[384,1024]{1,0:T(8,128)}) %reduce-scatter.5.cloned.1.call-update) | async-done | bytes 1572880 | tf_op jit(solution)/shard_map/reduce_scatter | solution.py:14
  713.4 1.5 convert_element_type.3
  714.9 0.0 copy-start
  714.9 0.4 convolution_bitcast_fusion
  715.4 0.9 copy.10
  716.3 0.0 reduce-scatter.7.cloned.1.call-update
  716.3 21.0 %reduce-scatter.7.cloned.1.call-done = f32[64,384]{1,0:T(8,128)} async-done(((f32[256,384]{1,0:T(8,128)}), f32[64,384]{1,0:T(8,128)}) %reduce-scatter.7.cloned.1.call-update) | async-done | bytes 98320
  737.3 1.0 copy.11
  738.3 0.0 copy-done.2
  738.3 0.1 broadcast_multiply_fusion
  738.4 0.8 copy.9
  739.2 0.0 copy-done
Async XLA Ops:
  7.2 485.5 %all-gather.2.cloned.1.call-start = ((), (), s32[]{:S(2)}) async-start(), calls=%async_computation.3 | async-start | bytes 28311552 | tf_op jit(solution)/shard_map/all_gather | solution.py:9
  7.9 705.5 %reduce-scatter.5.cloned.1.call-start = ((), (), s32[]{:S(2)}) async-start(), calls=%async_computation.4 | async-start | bytes 7864320 | tf_op jit(solution)/shard_map/reduce_scatter | solution.py:14
  656.3 0.8 copy-start.1
  656.3 82.0 %copy-start.2 = (f32[384]{0:T(512)S(1)}, f32[384]{0:T(512)}, u32[]{:S(2)}) copy-start(f32[384]{0:T(512)} %param.7) | copy-start | bytes 4612
  656.3 81.0 %reduce-scatter.7.cloned.1.call-start = ((), (), s32[]{:S(2)}) async-start(), calls=%async_computation.5 | async-start | bytes 491520
  714.9 24.3 %copy-start = (bf16[384,1024]{1,0:T(8,128)(2,1)}, bf16[384,1024]{1,0:T(8,128)(2,1)S(1)}, u32[]{:S(2)}) copy-start(bf16[384,1024]{1,0:T(8,128)(2,1)S(1)} %convert_element_type.3) | copy-start | bytes 2359300
Sparse Core Ops, SparseCore 0:
  9.5 483.0 all-gather.1
  656.4 56.9 reduce-scatter.4
  716.4 20.8 reduce-scatter.6
where the time goes:
time: 746 us
  waiting for transfers between devices  531 us (71%)
  blocking collectives  174 us (23%)
  matrix products  18.1 us (2%)
  between operations  13.8 us (2%)
    all_gather x1, waiting for transfers between devices, local(): lax.all_gather(train_grads, 'ex', axis=0, tiled=True)  485 us
    all_to_all x1, blocking collectives, local(): lax.all_to_all(columns, 'ex', split_axis=0, concat_axis=1, tiled=True)  143 us
    all_gather x1, blocking collectives, local(): lax.all_gather(test_features, 'ex', axis=0, tiled=True)  31.6 us
    reduce_scatter x1, waiting for transfers between devices, local(): lax.psum_scatter(partial_value, 'feat', scatter_dimension=1, tiled=True)  24.7 us
    unnamed x4, waiting for transfers between devices  21.7 us
    dot_general x1, matrix products, local(): jnp.dot(lax.all_gather(train_grads, 'ex', axis=0, tiled=True), projection...  17.7 us
  transfers between devices with their start and end apart: 3, of which 3 were waited for; matrix products, arithmetic and copies ran while one was open for 0% of the time, Pallas kernels for 0%

commit v1 on v0

v1 whole, which is shorter than its diff:
```python
import jax
import jax.numpy as jnp
from jax import lax
from jax.sharding import PartitionSpec as P


def solution(mesh):
    E, F = mesh.shape["ex"], mesh.shape["feat"]
    L = 2
    H = F // L
    X = E // F
    Q = X // H
    both = ("ex", "feat")

    def ex_of(h, l, x):
        return (h * L + l) * X + x

    coords = [(h, l, x) for h in range(H) for l in range(L) for x in range(X)]

    def shift_h(d):
        return [(ex_of(h, l, x), ex_of((h + d) % H, l, x)) for h, l, x in coords]

    def shift_l(d):
        return [(ex_of(h, l, x), ex_of(h, (l + d) % L, x)) for h, l, x in coords]

    def shift_x(d):
        return [(ex_of(h, l, x), ex_of(h, l, (x + d) % X)) for h, l, x in coords]

    def shift_c(d):
        return [(y * L + c, y * L + (c + d) % L) for y in range(H) for c in range(L)]

    def shift_y(d):
        return [(y * L + c, (y + d) % H * L + c) for y in range(H) for c in range(L)]

    def home(t, s):
        pairs = []
        for h, l, x in coords:
            for y in range(H):
                k = (y - h) % H
                dh, dx = (t + k) % H, k * Q + s
                for c in range(L):
                    src = ex_of(h, l, x) * F + y * L + c
                    dst = ex_of((h - dh) % H, l, (x - dx) % X) * F + h * L + c
                    pairs.append((src, dst))
        return pairs

    def mod(v, n):
        return lax.rem(v + 4 * n, n)

    def pick(options, index):
        out = options[0]
        for i in range(1, len(options)):
            out = jnp.where(index == i, options[i], out)
        return out

    def dot(a, b):
        return jnp.dot(a, b, preferred_element_type=jnp.float32)

    def local(a, b, test, weights):
        rows, cols = a.shape[0], b.shape[1]
        e, f = lax.axis_index("ex"), lax.axis_index("feat")
        h, l, x = lax.div(e, L * X), lax.rem(lax.div(e, X), L), lax.rem(e, X)
        y, c = lax.div(f, L), lax.rem(f, L)
        k = mod(y - h, H)

        r_cuts = [0, rows // 2, rows // 2 + rows // 3, rows]
        n_r = len(r_cuts) - 1
        if cols % 512 == 0:
            w, c_cuts = cols // 4, [0, 2, 3, 4]
        else:
            w, c_cuts = cols, [0, 1]
        n_c = len(c_cuts) - 1
        n_g = c_cuts[-1]

        def rows_of(v, i):
            return v[r_cuts[i] : r_cuts[i + 1]]

        a_in = [rows_of(a, i) for i in range(n_r)]
        b_in = [b[:, c_cuts[j] * w : c_cuts[j + 1] * w] for j in range(n_c)]
        far = [[lax.ppermute(p, "ex", shift_h(dh)) for p in a_in] for dh in range(1, H)]
        b_l = [[lax.ppermute(p, "ex", shift_l(dl)) for p in b_in] for dl in range(1, L)]
        near = [a] + [lax.ppermute(a, "ex", shift_x(dx)) for dx in range(1, X)]
        far_x = [
            [pieces]
            + [[lax.ppermute(p, "ex", shift_x(dx)) for p in pieces] for dx in range(1, X)]
            for pieces in far
        ]

        late, _ = lax.optimization_barrier((test, far[-1][-1] if far else test))
        tests = late
        for axis_shift, n in ((shift_h, H), (shift_l, L), (shift_x, X)):
            tests = jnp.stack(
                [tests] + [lax.ppermute(tests, "ex", axis_shift(d)) for d in range(1, n)]
            )
        tests = jnp.transpose(tests, (2, 1, 0, 3, 4))
        tests = tests.reshape(-1, tests.shape[-1])

        products = {}

        def product(dh, dx, dl, i, g):
            j = None if dl == 0 else next(n for n in range(n_c) if g < c_cuts[n + 1])
            piece = None if dh == 0 else i
            key = dh, dx, dl, piece, j
            if key not in products:
                lhs = near[dx] if dh == 0 else far_x[dh - 1][dx][i]
                products[key] = dot(lhs, b if dl == 0 else b_l[dl - 1][j])
            out = products[key]
            out = rows_of(out, i) if dh == 0 else out
            g = g if dl == 0 else g - c_cuts[j]
            return out[:, g * w : (g + 1) * w]

        got = {}
        gate = []

        def unit(blocks):
            n = sum(r_cuts[i + 1] - r_cuts[i] for i, g in blocks)

            taken = [
                [product(dh, dx, dl, i, g) for dl in range(L)]
                for dh in range(H)
                for dx in range(X)
                for i, g in blocks
            ]
            if gate:
                taken, _ = lax.optimization_barrier((taken, gate[-1]))

            def stack(d):
                return jnp.concatenate([pick(v, mod(l - c - d, L)) for v in taken], axis=0)

            sends = [stack(d) for d in range(1, L)]
            gate.append(sends)
            sent = [lax.ppermute(v, "feat", shift_c(d + 1)) for d, v in enumerate(sends)]
            total = stack(0)
            for s in sent:
                total = total + s
            total = total.reshape(H, H, Q * n, w)
            kept = pick([total[:, i] for i in range(H)], k)
            for d in range(1, H):
                out = pick([total[:, i] for i in range(H)], mod(k + d, H)).astype(jnp.bfloat16)
                kept = kept + lax.ppermute(out, "feat", shift_y(d)).astype(jnp.float32)
            final = kept.astype(jnp.bfloat16)
            for t in range(H):
                out = pick([final[i] for i in range(H)], mod(t + k, H))
                for s in range(Q):
                    res = lax.ppermute(out[s * n : (s + 1) * n], both, home(t, s))
                    r = 0
                    for i, g in blocks:
                        m = r_cuts[i + 1] - r_cuts[i]
                        got[t * Q + s, i, g] = res[r : r + m]
                        r += m

        done = []
        for j in range(n_c):
            for i in range(n_r):
                for g in range(c_cuts[j], c_cuts[j + 1]):
                    done.append((max(i, j * (n_r - 1) // max(n_c - 1, 1)), i, g))
        for stage in range(n_r):
            blocks = [(i, g) for s, i, g in done if s == stage]
            if blocks:
                unit(blocks)

        slots = [
            jnp.concatenate(
                [
                    jnp.concatenate([got[n, i, g] for g in range(n_g)], axis=1)
                    for i in range(n_r)
                ],
                axis=0,
            )
            for n in range(X)
        ]
        projected = []
        for kx in range(X):
            dx = mod(kx - x, X)
            t = mod(y - h - lax.div(dx, Q), H)
            projected.append(pick(slots, t * Q + lax.rem(dx, Q)))
        projected = jnp.concatenate(projected, axis=1)

        part = lax.dot_general(
            tests, projected, (((1,), (1,)), ((), ())), preferred_element_type=jnp.float32
        )
        part = part.reshape(H, L, part.shape[0] // F, part.shape[1])
        mine = pick([part[:, d] for d in range(L)], mod(l - c, L))
        for d in range(1, L):
            out = pick([part[:, i] for i in range(L)], mod(l - c - d, L))
            mine = mine + lax.ppermute(out, "feat", shift_c(d))
        inner = pick([mine[d] for d in range(H)], mod(h - y, H))
        for d in range(1, H):
            out = pick([mine[i] for i in range(H)], mod(h - y - d, H))
            inner = inner + lax.ppermute(out, "feat", shift_y(d))
        own = inner.shape[0] // X
        inner = jnp.concatenate(
            [
                pick([inner[d * own : (d + 1) * own] for d in range(X)], mod(x - kx, X))
                for kx in range(X)
            ],
            axis=0,
        )
        return inner * weights[None, :], projected

    return jax.shard_map(
        local,
        mesh=mesh,
        in_specs=(P("ex", "feat"), P("feat", "ex"), P("ex", "feat"), P("ex")),
        out_specs=(P("feat", "ex"), P("ex", "feat")),
        check_vma=False,
    )
```

time: 746 us -> 299 us (0.40)
  waiting for transfers between devices: 531 us -> 196 us
  blocking collectives: 174 us -> 0 us
  starting transfers between devices: 0.12 us -> 42.7 us
  matrix products: 18.1 us -> 38.7 us
  between operations: 13.8 us -> 2.04 us
  local copies, waits for them, and re-layouts: 6.85 us -> 16.4 us
    all_gather x1 -> x0, waiting for transfers between devices: 485 us -> none  [local(): lax.all_gather(train_grads, 'ex', axis=0, tiled=True)]
    ppermute x0 -> x27, waiting for transfers between devices: none -> 196 us  [the longest x3 62.3 us: local(): lax.ppermute(p, 'ex', shift_h(dh))]
    all_to_all x1 -> x0, blocking collectives: 143 us -> none  [local(): lax.all_to_all(columns, 'ex', split_axis=0, concat_axis=1, tiled=True)]
    ppermute x0 -> x27, starting transfers between devices: none -> 42.7 us  [the longest x6 9.96 us: unit(): res = lax.ppermute(out[s * n:(s + 1) * n], both, home(t, s))]
    all_gather x1 -> x0, blocking collectives: 31.6 us -> none  [local(): lax.all_gather(test_features, 'ex', axis=0, tiled=True)]
    reduce_scatter x1 -> x0, waiting for transfers between devices: 24.7 us -> none  [local(): lax.psum_scatter(partial_value, 'feat', scatter_dimension=1, tiled=True)]
    unnamed x4 -> x0, waiting for transfers between devices: 21.7 us -> none
    dot_general x2 -> x33, matrix products: 18.1 us -> 38.7 us  [the longest x32 38.2 us: dot(): return jnp.dot(a, b, preferred_element_type=jnp.float32)]
  transfers between devices with their start and end apart: 3 -> 27, of which waited for: 3 -> 13; matrix products, arithmetic and copies ran while one was open for 0% -> 18% of each run, Pallas kernels for 0% -> 0%
where the time goes in v1:
time: 299 us
  waiting for transfers between devices  196 us (66%)
  starting transfers between devices  42.7 us (14%)
  matrix products  38.7 us (13%)
  local copies, waits for them, and re-layouts  16.4 us (5%)
    ppermute x3, waiting for transfers between devices, local(): lax.ppermute(p, 'ex', shift_h(dh))  62.3 us
    ppermute x3, waiting for transfers between devices, local(): lax.ppermute(tests, 'ex', axis_shift(d))  59 us
    ppermute x3, waiting for transfers between devices, local(): lax.ppermute(p, 'ex', shift_l(dl))  41.7 us
    dot_general x32, matrix products, dot(): return jnp.dot(a, b, preferred_element_type=jnp.float32)  38.2 us
    ppermute x3, waiting for transfers between devices, unit(): kept = kept + lax.ppermute(out, 'feat', shift_y(d)).astype(jnp.float32)  12.9 us
    ppermute x3, waiting for transfers between devices, local(): lax.ppermute(p, 'ex', shift_x(dx))  10 us
    ppermute x6, starting transfers between devices, unit(): res = lax.ppermute(out[s * n:(s + 1) * n], both, home(t, s))  9.96 us
    ppermute x3, starting transfers between devices, unit(): kept = kept + lax.ppermute(out, 'feat', shift_y(d)).astype(jnp.float32)  9.2 us
  transfers between devices with their start and end apart: 27, of which 13 were waited for; matrix products, arithmetic and copies ran while one was open for 18% of the time, Pallas kernels for 0%

profile of v1, /device:TPU:0, one launch (start us, length us, event | category | flops | bytes accessed | tf_op | source)
XLA Modules:
  0.0 298.5 jit_solution(4419377677725565961)
XLA Ops:
  0.6 3.0 %collective-permute-start.5 = (bf16[384,4096]{1,0:T(8,128)(2,1)}, bf16[384,4096]{1,0:T(8,128)(2,1)}, u32[]{:S(2)}, u32[]{:S(2)}) collective-permute-start(bf16[384,4096]{1,0:T(8,128)(2,1)} %param.4), channel_id=1, source_target_pairs={{0,4},{4,0},{8,12},{12,8},{16,20},{20,16},{24,28},{28,24},{1,5},{5... | collective-permute-start | bytes 9437192 | tf_op jit(solution)/shard_map/ppermute | solution.py:82
  3.7 1.9 slice.486
  5.6 2.6 collective-permute-start
  8.2 2.4 slice.528
  11.0 2.8 slice.496
  13.8 2.6 collective-permute-start.6
  16.4 1.5 fusion.12
  17.9 1.6 collective-permute-start.17
  19.5 1.8 fusion.36
  22.2 3.1 %slice.487 = bf16[4096,256]{1,0:T(8,128)(2,1)} slice(bf16[4096,512]{1,0:T(8,128)(2,1)} %param.5), slice={[0:4096], [0:256]} | slice | bytes 4194304 | tf_op jit(solution)/shard_map/slice | solution.py:79
  25.3 1.0 fusion.14
  26.3 62.3 %collective-permute-done = bf16[64,4096]{1,0:T(8,128)(2,1)S(1)} collective-permute-done((bf16[64,4096]{1,0:T(8,128)(2,1)}, bf16[64,4096]{1,0:T(8,128)(2,1)S(1)}, u32[]{:S(2)}, u32[]{:S(2)}) %collective-permute-start) | collective-permute-done | bytes 524320 | tf_op jit(solution)/shard_map/ppermute | solution.py:80
  88.6 3.2 %fusion.55 = f32[64,512]{1,0:T(8,128)S(1)} fusion(bf16[64,4096]{1,0:T(8,128)(2,1)S(1)} %collective-permute-done, bf16[4096,512]{1,0:T(8,128)(2,1)} %param.5), kind=kOutput, calls=%fused_computation.184 | convolution fusion | flops 268435456 | bytes 4849664 | tf_op jit(solution)/shard_map/dot_general | solution.py:57
  91.8 54.7 %collective-permute-done.1 = bf16[32,1024]{1,0:T(8,128)(2,1)S(1)} collective-permute-done((bf16[32,1024]{1,0:T(8,128)(2,1)S(1)}, bf16[32,1024]{1,0:T(8,128)(2,1)S(1)}, u32[]{:S(2)}, u32[]{:S(2)}) %collective-permute-start.1) | collective-permute-done | bytes 65568 | tf_op jit(solution)/shard_map/ppermute | solution.py:93
  147.3 4.3 %collective-permute-done.2 = bf16[2,32,1024]{2,1,0:T(8,128)(2,1)S(1)} collective-permute-done((bf16[2,32,1024]{2,1,0:T(8,128)(2,1)S(1)}, bf16[2,32,1024]{2,1,0:T(8,128)(2,1)S(1)}, u32[]{:S(2)}, u32[]{:S(2)}) %collective-permute-start.2) | collective-permute-done | bytes 131104 | tf_op jit(solution)/shard_map/ppermute | solution.py:93
  151.6 1.1 collective-permute-start.11
  153.3 2.1 fusion.45
  155.5 10.0 %collective-permute-done.18 = bf16[64,4096]{1,0:T(8,128)(2,1)S(1)} collective-permute-done((bf16[64,4096]{1,0:T(8,128)(2,1)S(1)}, bf16[64,4096]{1,0:T(8,128)(2,1)S(1)}, u32[]{:S(2)}, u32[]{:S(2)}) %collective-permute-start.18) | collective-permute-done | bytes 524320 | tf_op jit(solution)/shard_map/ppermute | solution.py:85
  166.7 1.0 fusion.53
  168.5 9.1 %collective-permute-done.11 = bf16[4096,128]{1,0:T(8,128)(2,1)S(1)} collective-permute-done((bf16[4096,128]{1,0:T(8,128)(2,1)S(1)}, bf16[4096,128]{1,0:T(8,128)(2,1)S(1)}, u32[]{:S(2)}, u32[]{:S(2)}) %collective-permute-start.11) | collective-permute-done | bytes 1048608 | tf_op jit(solution)/shard_map/ppermute | solution.py:81
  177.6 1.0 fusion.43
  180.4 1.6 fusion.59
  182.1 1.7 fusion.48
  183.7 1.6 collective-permute-start.7
  186.5 1.0 fusion.40
  187.5 32.6 %collective-permute-done.4 = bf16[4096,256]{1,0:T(8,128)(2,1)S(1)} collective-permute-done((bf16[4096,256]{1,0:T(8,128)(2,1)S(1)}, bf16[4096,256]{1,0:T(8,128)(2,1)S(1)}, u32[]{:S(2)}, u32[]{:S(2)}) %collective-permute-start.4) | collective-permute-done | bytes 2097184 | tf_op jit(solution)/shard_map/ppermute | solution.py:81
  220.1 1.0 fusion.35
  222.1 1.7 fusion.46
  225.1 0.9 fusion.49
  227.6 2.9 fusion.44
  230.5 2.9 fusion.54
  233.4 3.7 %fusion.38 = f32[384,512]{1,0:T(8,128)S(1)} fusion(bf16[384,4096]{1,0:T(8,128)(2,1)} %collective-permute-done.5, bf16[4096,512]{1,0:T(8,128)(2,1)S(1)} %copy-done.1), kind=kOutput, calls=%fused_computation.167 | convolution fusion | flops 1610612736 | bytes 8126464 | tf_op jit(solution)/shard_map/dot_general | solution.py:57
  237.2 2.9 fusion.37
  240.4 1.0 fusion.42
  246.4 1.6 collective-permute-start.9
  248.1 5.3 %collective-permute-done.9 = bf16[2,384,128]{2,1,0:T(8,128)(2,1)S(1)} collective-permute-done((bf16[2,384,128]{2,1,0:T(8,128)(2,1)S(1)}, bf16[2,384,128]{2,1,0:T(8,128)(2,1)S(1)}, u32[]{:S(2)}, u32[]{:S(2)}) %collective-permute-start.9) | collective-permute-done | bytes 196640 | tf_op jit(solution)/shard_map/ppermute | solution.py:140
  253.5 3.7 %collective-permute-start.10 = (bf16[384,128]{1,0:T(8,128)(2,1)S(1)}, bf16[384,128]{1,0:T(8,128)(2,1)S(1)}, u32[]{:S(2)}, u32[]{:S(2)}) collective-permute-start(bf16[384,128]{1,0:T(8,128)(2,1)S(1)} %get-tuple-element.220), channel_id=1, source_target_pairs={{0,16},{1,17},{2,4},{3,5},{4,20},{5,21},{6,0},{7,1},{8,24},{9,25},... | collective-permute-start | bytes 294920 | tf_op jit(solution)/shard_map/ppermute | solution.py:145
  258.0 1.4 collective-permute-done.10
  259.6 3.8 %collective-permute-start.15 = (bf16[2,576,128]{2,1,0:T(8,128)(2,1)S(1)}, bf16[2,576,128]{2,1,0:T(8,128)(2,1)S(1)}, u32[]{:S(2)}, u32[]{:S(2)}) collective-permute-start(bf16[2,576,128]{2,1,0:T(8,128)(2,1)S(1)} %fusion.5), channel_id=1, source_target_pairs={{0,2},{1,3},{2,0},{3,1},{4,6},{5,7},{6,4},{7,5},{8,10},{9,11},{10,... | collective-permute-start | bytes 884744 | tf_op jit(solution)/shard_map/ppermute | solution.py:140
  263.6 3.8 %collective-permute-start.20 = (bf16[2,576,128]{2,1,0:T(8,128)(2,1)S(1)}, bf16[2,576,128]{2,1,0:T(8,128)(2,1)S(1)}, u32[]{:S(2)}, u32[]{:S(2)}) collective-permute-start(bf16[2,576,128]{2,1,0:T(8,128)(2,1)S(1)} %fusion.6), channel_id=1, source_target_pairs={{0,2},{1,3},{2,0},{3,1},{4,6},{5,7},{6,4},{7,5},{8,10},{9,11},{10,... | collective-permute-start | bytes 884744 | tf_op jit(solution)/shard_map/ppermute | solution.py:140
  267.4 3.8 %collective-permute-done.15 = bf16[2,576,128]{2,1,0:T(8,128)(2,1)S(1)} collective-permute-done((bf16[2,576,128]{2,1,0:T(8,128)(2,1)S(1)}, bf16[2,576,128]{2,1,0:T(8,128)(2,1)S(1)}, u32[]{:S(2)}, u32[]{:S(2)}) %collective-permute-start.15) | collective-permute-done | bytes 294944 | tf_op jit(solution)/shard_map/ppermute | solution.py:140
  271.4 2.8 collective-permute-start.16
  274.9 3.8 %collective-permute-done.20 = bf16[2,576,128]{2,1,0:T(8,128)(2,1)S(1)} collective-permute-done((bf16[2,576,128]{2,1,0:T(8,128)(2,1)S(1)}, bf16[2,576,128]{2,1,0:T(8,128)(2,1)S(1)}, u32[]{:S(2)}, u32[]{:S(2)}) %collective-permute-start.20) | collective-permute-done | bytes 294944 | tf_op jit(solution)/shard_map/ppermute | solution.py:140
  278.8 1.4 collective-permute-start.21
  281.0 3.9 %collective-permute-done.21 = bf16[576,128]{1,0:T(8,128)(2,1)S(1)} collective-permute-done((bf16[576,128]{1,0:T(8,128)(2,1)S(1)}, bf16[576,128]{1,0:T(8,128)(2,1)S(1)}, u32[]{:S(2)}, u32[]{:S(2)}) %collective-permute-start.21) | collective-permute-done | bytes 147488 | tf_op jit(solution)/shard_map/ppermute | solution.py:145
  286.0 1.4 collective-permute-done.25
  287.4 7.3 %collective-permute-start.26 = (f32[64,384]{1,0:T(8,128)S(1)}, f32[64,384]{1,0:T(8,128)S(1)}, u32[]{:S(2)}, u32[]{:S(2)}) collective-permute-start(f32[64,384]{1,0:T(8,128)S(1)} %select_bitcast_fusion.5), channel_id=1, source_target_pairs={{0,2},{1,3},{2,0},{3,1},{4,6},{5,7},{6,4},{7,5},{8,10},{9,11},{10,... | collective-permute-start | bytes 294920 | tf_op jit(solution)/shard_map/ppermute | solution.py:190
  294.7 3.1 %collective-permute-done.26 = f32[64,384]{1,0:T(8,128)S(1)} collective-permute-done((f32[64,384]{1,0:T(8,128)S(1)}, f32[64,384]{1,0:T(8,128)S(1)}, u32[]{:S(2)}, u32[]{:S(2)}) %collective-permute-start.26) | collective-permute-done | bytes 98336 | tf_op jit(solution)/shard_map/ppermute | solution.py:190
  (203 shorter events, 20.7 us)
Async XLA Ops:
  0.6 226.9 %collective-permute-start.5 = (bf16[384,4096]{1,0:T(8,128)(2,1)}, bf16[384,4096]{1,0:T(8,128)(2,1)}, u32[]{:S(2)}, u32[]{:S(2)}) collective-permute-start(bf16[384,4096]{1,0:T(8,128)(2,1)} %param.4), channel_id=1, source_target_pairs={{0,4},{4,0},{8,12},{12,8},{16,20},{20,16},{24,28},{28,24},{1,5},{5... | collective-permute-start | bytes 9437192 | tf_op jit(solution)/shard_map/ppermute | solution.py:82
  5.6 83.0 %collective-permute-start = (bf16[64,4096]{1,0:T(8,128)(2,1)}, bf16[64,4096]{1,0:T(8,128)(2,1)S(1)}, u32[]{:S(2)}, u32[]{:S(2)}) collective-permute-start(bf16[64,4096]{1,0:T(8,128)(2,1)} %slice.486), channel_id=1, source_target_pairs={{0,16},{4,20},{8,24},{12,28},{16,0},{20,4},{24,8},{28,12},{1,17},{... | collective-permute-start | bytes 1572872 | tf_op jit(solution)/shard_map/ppermute | solution.py:80
  8.2 8.2 %copy-start = (bf16[4096,512]{1,0:T(8,128)(2,1)S(1)}, bf16[4096,512]{1,0:T(8,128)(2,1)}, u32[]{:S(2)}) copy-start(bf16[4096,512]{1,0:T(8,128)(2,1)} %param.5) | copy-start | bytes 12582916
  10.6 142.1 %collective-permute-start.12 = (bf16[128,4096]{1,0:T(8,128)(2,1)}, bf16[128,4096]{1,0:T(8,128)(2,1)}, u32[]{:S(2)}, u32[]{:S(2)}) collective-permute-start(bf16[128,4096]{1,0:T(8,128)(2,1)} %slice.528), channel_id=1, source_target_pairs={{0,16},{4,20},{8,24},{12,28},{16,0},{20,4},{24,8},{28,12},{1,17},{... | collective-permute-start | bytes 3145736 | tf_op jit(solution)/shard_map/ppermute | solution.py:80
  13.8 5.7 %copy-start.2 = (bf16[384,4096]{1,0:T(8,128)(2,1)S(1)}, bf16[384,4096]{1,0:T(8,128)(2,1)}, u32[]{:S(2)}) copy-start(bf16[384,4096]{1,0:T(8,128)(2,1)} %param.4) | copy-start | bytes 9437188
  13.8 169.9 %collective-permute-start.6 = (bf16[192,4096]{1,0:T(8,128)(2,1)}, bf16[192,4096]{1,0:T(8,128)(2,1)S(1)}, u32[]{:S(2)}, u32[]{:S(2)}) collective-permute-start(bf16[192,4096]{1,0:T(8,128)(2,1)} %slice.496), channel_id=1, source_target_pairs={{0,16},{4,20},{8,24},{12,28},{16,0},{20,4},{24,8},{28,12},{1,17},{... | collective-permute-start | bytes 4718600 | tf_op jit(solution)/shard_map/ppermute | solution.py:80
  17.9 147.9 %collective-permute-start.17 = (bf16[4096,128]{1,0:T(8,128)(2,1)}, bf16[4096,128]{1,0:T(8,128)(2,1)S(1)}, u32[]{:S(2)}, u32[]{:S(2)}) collective-permute-start(bf16[4096,128]{1,0:T(8,128)(2,1)} %get-tuple-element.164), channel_id=1, source_target_pairs={{0,8},{4,12},{8,0},{12,4},{16,24},{20,28},{24,16},{28,20},{1,9},{5... | collective-permute-start | bytes 3145736 | tf_op jit(solution)/shard_map/ppermute | solution.py:81
  22.2 66.4 %copy-start.13 = (bf16[32,1024]{1,0:T(8,128)(2,1)S(1)}, bf16[32,1024]{1,0:T(8,128)(2,1)}, u32[]{:S(2)}) copy-start(bf16[32,1024]{1,0:T(8,128)(2,1)} %param.6) | copy-start | bytes 196612
  26.3 125.3 %copy-start.8 = (bf16[4096,128]{1,0:T(8,128)(2,1)S(1)}, bf16[4096,128]{1,0:T(8,128)(2,1)}, u32[]{:S(2)}) copy-start(bf16[4096,128]{1,0:T(8,128)(2,1)} %get-tuple-element.165) | copy-start | bytes 3145732
  88.6 57.9 %collective-permute-start.1 = (bf16[32,1024]{1,0:T(8,128)(2,1)S(1)}, bf16[32,1024]{1,0:T(8,128)(2,1)S(1)}, u32[]{:S(2)}, u32[]{:S(2)}) collective-permute-start(bf16[32,1024]{1,0:T(8,128)(2,1)S(1)} %copy-done.13), channel_id=1, source_target_pairs={{0,16},{4,20},{8,24},{12,28},{16,0},{20,4},{24,8},{28,12},{1,17},{... | collective-permute-start | bytes 196616 | tf_op jit(solution)/shard_map/ppermute | solution.py:93
  88.6 64.7 %copy-start.1 = (bf16[4096,512]{1,0:T(8,128)(2,1)S(1)}, bf16[4096,512]{1,0:T(8,128)(2,1)}, u32[]{:S(2)}) copy-start(bf16[4096,512]{1,0:T(8,128)(2,1)} %param.5) | copy-start | bytes 12582916
  146.5 5.0 %collective-permute-start.2 = (bf16[2,32,1024]{2,1,0:T(8,128)(2,1)S(1)}, bf16[2,32,1024]{2,1,0:T(8,128)(2,1)S(1)}, u32[]{:S(2)}, u32[]{:S(2)}) collective-permute-start(bf16[2,32,1024]{2,1,0:T(8,128)(2,1)S(1)} %get-tuple-element.297), channel_id=1, source_target_pairs={{0,8},{4,12},{8,0},{12,4},{16,24},{20,28},{24,16},{28,20},{1,9},{5... | collective-permute-start | bytes 393224 | tf_op jit(solution)/shard_map/ppermute | solution.py:93
  151.6 26.0 %collective-permute-start.11 = (bf16[4096,128]{1,0:T(8,128)(2,1)S(1)}, bf16[4096,128]{1,0:T(8,128)(2,1)S(1)}, u32[]{:S(2)}, u32[]{:S(2)}) collective-permute-start(bf16[4096,128]{1,0:T(8,128)(2,1)S(1)} %copy-done.8), channel_id=1, source_target_pairs={{0,8},{4,12},{8,0},{12,4},{16,24},{20,28},{24,16},{28,20},{1,9},{5... | collective-permute-start | bytes 3145736 | tf_op jit(solution)/shard_map/ppermute | solution.py:81
  152.7 12.8 %copy-start.5 = (bf16[4096,256]{1,0:T(8,128)(2,1)S(1)}, bf16[4096,256]{1,0:T(8,128)(2,1)}, u32[]{:S(2)}) copy-start(bf16[4096,256]{1,0:T(8,128)(2,1)} %slice.487) | copy-start | bytes 6291460
  152.7 12.8 %collective-permute-start.18 = (bf16[64,4096]{1,0:T(8,128)(2,1)S(1)}, bf16[64,4096]{1,0:T(8,128)(2,1)S(1)}, u32[]{:S(2)}, u32[]{:S(2)}) collective-permute-start(bf16[64,4096]{1,0:T(8,128)(2,1)S(1)} %collective-permute-done), channel_id=1, source_target_pairs={{0,4},{4,0},{8,12},{12,8},{16,20},{20,16},{24,28},{28,24},{1,5},{5... | collective-permute-start | bytes 1572872 | tf_op jit(solution)/shard_map/ppermute | solution.py:85
  153.3 13.3 %copy-start.3 = (bf16[384,4096]{1,0:T(8,128)(2,1)S(1)}, bf16[384,4096]{1,0:T(8,128)(2,1)}, u32[]{:S(2)}) copy-start(bf16[384,4096]{1,0:T(8,128)(2,1)} %param.4) | copy-start | bytes 9437188
  165.5 54.6 %collective-permute-start.4 = (bf16[4096,256]{1,0:T(8,128)(2,1)S(1)}, bf16[4096,256]{1,0:T(8,128)(2,1)S(1)}, u32[]{:S(2)}, u32[]{:S(2)}) collective-permute-start(bf16[4096,256]{1,0:T(8,128)(2,1)S(1)} %copy-done.5), channel_id=1, source_target_pairs={{0,8},{4,12},{8,0},{12,4},{16,24},{20,28},{24,16},{28,20},{1,9},{5... | collective-permute-start | bytes 6291464 | tf_op jit(solution)/shard_map/ppermute | solution.py:81
  165.8 91.4 %collective-permute-start.3 = (bf16[2,2,32,1024]{3,2,1,0:T(8,128)(2,1)S(1)}, bf16[2,2,32,1024]{3,2,1,0:T(8,128)(2,1)S(1)}, u32[]{:S(2)}, u32[]{:S(2)}) collective-permute-start(bf16[2,2,32,1024]{3,2,1,0:T(8,128)(2,1)S(1)} %get-tuple-element.219), channel_id=1, source_target_pairs={{0,4},{4,0},{8,12},{12,8},{16,20},{20,16},{24,28},{28,24},{1,5},{5... | collective-permute-start | bytes 786440 | tf_op jit(solution)/shard_map/ppermute | solution.py:93
  167.7 11.2 %copy-start.9 = (f32[384,128]{1,0:T(8,128)}, f32[384,128]{1,0:T(8,128)S(1)}, u32[]{:S(2)}) copy-start(f32[384,128]{1,0:T(8,128)S(1)} %fusion.53) | copy-start | bytes 589828
  179.3 44.6 %collective-permute-start.13 = (bf16[128,4096]{1,0:T(8,128)(2,1)}, bf16[128,4096]{1,0:T(8,128)(2,1)S(1)}, u32[]{:S(2)}, u32[]{:S(2)}) collective-permute-start(bf16[128,4096]{1,0:T(8,128)(2,1)} %collective-permute-done.12), channel_id=1, source_target_pairs={{0,4},{4,0},{8,12},{12,8},{16,20},{20,16},{24,28},{28,24},{1,5},{5... | collective-permute-start | bytes 3145736 | tf_op jit(solution)/shard_map/ppermute | solution.py:85
  183.7 56.6 %collective-permute-start.7 = (bf16[192,4096]{1,0:T(8,128)(2,1)S(1)}, bf16[192,4096]{1,0:T(8,128)(2,1)S(1)}, u32[]{:S(2)}, u32[]{:S(2)}) collective-permute-start(bf16[192,4096]{1,0:T(8,128)(2,1)S(1)} %collective-permute-done.6), channel_id=1, source_target_pairs={{0,4},{4,0},{8,12},{12,8},{16,20},{20,16},{24,28},{28,24},{1,5},{5... | collective-permute-start | bytes 4718600 | tf_op jit(solution)/shard_map/ppermute | solution.py:85
  223.8 1.1 copy-start.7
  230.4 3.0 copy-start.11
  233.4 3.8 %copy-start.12 = (f32[384,128]{1,0:T(8,128)}, f32[384,128]{1,0:T(8,128)S(1)}, u32[]{:S(2)}) copy-start(f32[384,128]{1,0:T(8,128)S(1)} %fusion.54) | copy-start | bytes 589828
  242.1 4.2 %collective-permute-start.8 = (f32[1536,128]{1,0:T(8,128)S(1)}, f32[1536,128]{1,0:T(8,128)S(1)}, u32[]{:S(2)}, u32[]{:S(2)}) collective-permute-start(f32[1536,128]{1,0:T(8,128)S(1)} %constant_dynamic-update-slice_fusion.8), channel_id=1, source_target_pairs={{0,1},{1,0},{2,3},{3,2},{4,5},{5,4},{6,7},{7,6},{8,9},{9,8},{10,11... | collective-permute-start | bytes 2359304 | tf_op jit(solution)/shard_map/ppermute | solution.py:132
  242.7 0.9 slice-start.8
  242.7 0.9 slice-start.7
  243.9 1.3 slice-start.3
  243.9 1.3 slice-start.2
  243.9 1.3 slice-start.1
  243.9 1.3 slice-start
  243.9 15.5 %collective-permute-start.14 = (f32[2304,128]{1,0:T(8,128)S(1)}, f32[2304,128]{1,0:T(8,128)S(1)}, u32[]{:S(2)}, u32[]{:S(2)}) collective-permute-start(f32[2304,128]{1,0:T(8,128)S(1)} %get-tuple-element.253), channel_id=1, source_target_pairs={{0,1},{1,0},{2,3},{3,2},{4,5},{5,4},{6,7},{7,6},{8,9},{9,8},{10,11... | collective-permute-start | bytes 3538952 | tf_op jit(solution)/shard_map/ppermute | solution.py:132
  245.1 0.9 slice-start.10
  245.1 0.9 slice-start.9
  246.4 6.9 %collective-permute-start.9 = (bf16[2,384,128]{2,1,0:T(8,128)(2,1)S(1)}, bf16[2,384,128]{2,1,0:T(8,128)(2,1)S(1)}, u32[]{:S(2)}, u32[]{:S(2)}) collective-permute-start(bf16[2,384,128]{2,1,0:T(8,128)(2,1)S(1)} %fusion.7), channel_id=1, source_target_pairs={{0,2},{1,3},{2,0},{3,1},{4,6},{5,7},{6,4},{7,5},{8,10},{9,11},{10,... | collective-permute-start | bytes 589832 | tf_op jit(solution)/shard_map/ppermute | solution.py:140
  248.0 15.4 %collective-permute-start.19 = (f32[2304,128]{1,0:T(8,128)S(1)}, f32[2304,128]{1,0:T(8,128)S(1)}, u32[]{:S(2)}, u32[]{:S(2)}) collective-permute-start(f32[2304,128]{1,0:T(8,128)S(1)} %get-tuple-element.304), channel_id=1, source_target_pairs={{0,1},{1,0},{2,3},{3,2},{4,5},{5,4},{6,7},{7,6},{8,9},{9,8},{10,11... | collective-permute-start | bytes 3538952 | tf_op jit(solution)/shard_map/ppermute | solution.py:132
  253.5 5.9 %collective-permute-start.10 = (bf16[384,128]{1,0:T(8,128)(2,1)S(1)}, bf16[384,128]{1,0:T(8,128)(2,1)S(1)}, u32[]{:S(2)}, u32[]{:S(2)}) collective-permute-start(bf16[384,128]{1,0:T(8,128)(2,1)S(1)} %get-tuple-element.220), channel_id=1, source_target_pairs={{0,16},{1,17},{2,4},{3,5},{4,20},{5,21},{6,0},{7,1},{8,24},{9,25},... | collective-permute-start | bytes 294920 | tf_op jit(solution)/shard_map/ppermute | solution.py:145
  257.3 6.1 %collective-permute-start.22 = (bf16[384,128]{1,0:T(8,128)(2,1)S(1)}, bf16[384,128]{1,0:T(8,128)(2,1)S(1)}, u32[]{:S(2)}, u32[]{:S(2)}) collective-permute-start(bf16[384,128]{1,0:T(8,128)(2,1)S(1)} %get-tuple-element.221), channel_id=1, source_target_pairs={{0,0},{1,1},{2,20},{3,21},{4,4},{5,5},{6,16},{7,17},{8,8},{9,9},{1... | collective-permute-start | bytes 294920 | tf_op jit(solution)/shard_map/ppermute | solution.py:145
  259.6 11.6 %collective-permute-start.15 = (bf16[2,576,128]{2,1,0:T(8,128)(2,1)S(1)}, bf16[2,576,128]{2,1,0:T(8,128)(2,1)S(1)}, u32[]{:S(2)}, u32[]{:S(2)}) collective-permute-start(bf16[2,576,128]{2,1,0:T(8,128)(2,1)S(1)} %fusion.5), channel_id=1, source_target_pairs={{0,2},{1,3},{2,0},{3,1},{4,6},{5,7},{6,4},{7,5},{8,10},{9,11},{10,... | collective-permute-start | bytes 884744 | tf_op jit(solution)/shard_map/ppermute | solution.py:140
  263.6 15.1 %collective-permute-start.20 = (bf16[2,576,128]{2,1,0:T(8,128)(2,1)S(1)}, bf16[2,576,128]{2,1,0:T(8,128)(2,1)S(1)}, u32[]{:S(2)}, u32[]{:S(2)}) collective-permute-start(bf16[2,576,128]{2,1,0:T(8,128)(2,1)S(1)} %fusion.6), channel_id=1, source_target_pairs={{0,2},{1,3},{2,0},{3,1},{4,6},{5,7},{6,4},{7,5},{8,10},{9,11},{10,... | collective-permute-start | bytes 884744 | tf_op jit(solution)/shard_map/ppermute | solution.py:140
  271.4 9.5 %collective-permute-start.16 = (bf16[576,128]{1,0:T(8,128)(2,1)S(1)}, bf16[576,128]{1,0:T(8,128)(2,1)S(1)}, u32[]{:S(2)}, u32[]{:S(2)}) collective-permute-start(bf16[576,128]{1,0:T(8,128)(2,1)S(1)} %get-tuple-element.206), channel_id=1, source_target_pairs={{0,16},{1,17},{2,4},{3,5},{4,20},{5,21},{6,0},{7,1},{8,24},{9,25},... | collective-permute-start | bytes 442376 | tf_op jit(solution)/shard_map/ppermute | solution.py:145
  274.2 6.7 %collective-permute-start.23 = (bf16[576,128]{1,0:T(8,128)(2,1)S(1)}, bf16[576,128]{1,0:T(8,128)(2,1)S(1)}, u32[]{:S(2)}, u32[]{:S(2)}) collective-permute-start(bf16[576,128]{1,0:T(8,128)(2,1)S(1)} %get-tuple-element.207), channel_id=1, source_target_pairs={{0,0},{1,1},{2,20},{3,21},{4,4},{5,5},{6,16},{7,17},{8,8},{9,9},{1... | collective-permute-start | bytes 442376 | tf_op jit(solution)/shard_map/ppermute | solution.py:145
  278.8 6.1 %collective-permute-start.21 = (bf16[576,128]{1,0:T(8,128)(2,1)S(1)}, bf16[576,128]{1,0:T(8,128)(2,1)S(1)}, u32[]{:S(2)}, u32[]{:S(2)}) collective-permute-start(bf16[576,128]{1,0:T(8,128)(2,1)S(1)} %get-tuple-element.208), channel_id=1, source_target_pairs={{0,16},{1,17},{2,4},{3,5},{4,20},{5,21},{6,0},{7,1},{8,24},{9,25},... | collective-permute-start | bytes 442376 | tf_op jit(solution)/shard_map/ppermute | solution.py:145
  280.2 4.7 %collective-permute-start.24 = (bf16[576,128]{1,0:T(8,128)(2,1)S(1)}, bf16[576,128]{1,0:T(8,128)(2,1)S(1)}, u32[]{:S(2)}, u32[]{:S(2)}) collective-permute-start(bf16[576,128]{1,0:T(8,128)(2,1)S(1)} %get-tuple-element.209), channel_id=1, source_target_pairs={{0,0},{1,1},{2,20},{3,21},{4,4},{5,5},{6,16},{7,17},{8,8},{9,9},{1... | collective-permute-start | bytes 442376 | tf_op jit(solution)/shard_map/ppermute | solution.py:145
  285.3 2.1 copy-start.4
  285.8 12.0 %copy-start.14 = (f32[384]{0:T(512)S(1)}, f32[384]{0:T(512)}, u32[]{:S(2)}) copy-start(f32[384]{0:T(512)} %param.7) | copy-start | bytes 4612
  285.9 1.5 collective-permute-start.25
  287.4 10.4 %collective-permute-start.26 = (f32[64,384]{1,0:T(8,128)S(1)}, f32[64,384]{1,0:T(8,128)S(1)}, u32[]{:S(2)}, u32[]{:S(2)}) collective-permute-start(f32[64,384]{1,0:T(8,128)S(1)} %select_bitcast_fusion.5), channel_id=1, source_target_pairs={{0,2},{1,3},{2,0},{3,1},{4,6},{5,7},{6,4},{7,5},{8,10},{9,11},{10,... | collective-permute-start | bytes 294920 | tf_op jit(solution)/shard_map/ppermute | solution.py:190
  (6 other events, 5.0 us)
